TPU v7x, 32 devices: a whole 2x2x4 slice. The times are simulated.
32 devices in a mesh: grp: 8 (over z, y), mem: 4 (over x, core).
Axes of the slice: x: 2, y: 2, z: 4, core: 2. Of those that a mesh axis runs over, the one named last changes fastest.
Arguments:
- codes: bfloat16 [8192, 1024], P(('grp', 'mem')), as said below
- scales: float32 [8192, 8], P(('grp', 'mem')), may hold values from 0.2 to 2
- cluster_id: int32 [8192], P(('grp', 'mem')), may hold values from 0 to 63, as said below
Outputs:
- smoothed: bfloat16 [8192, 1024], P(('grp', 'mem'))
- dup_mass: bfloat16 [8192], P(('grp', 'mem'))
Inputs may be any that keep to these rules, and one draw needn't show every extreme that they name: `cluster_id`: cluster c belongs to owner group c mod 8. Among the 256 documents of one device, at most 40 belong to clusters of any one owner group, and at most 20 to any one cluster; for each index along mem, some owner group gets exactly 40 from every device of that index, and some cluster of that group exactly 20 from every device of that index. `codes`: documents of one cluster lie near a common direction.
All inputs are finite; a program needn't handle non-finite values.
Results may differ from a plain program's by a relative error of at most 0.0034.
Values may be sent and summed in bfloat16 or wider, within the bound.
No kernel may reach another device: no remote copies, remote signals or barrier semaphores. Data moves between devices by JAX's collectives and lax.ppermute only.
A program may use at most 64 MiB of HBM per device.

v0:
```python
import jax
import jax.numpy as jnp
from jax import lax
from jax.sharding import PartitionSpec as P

CAP = 40


def embed(codes, scales):
    rows, width = codes.shape
    nblk = scales.shape[1]
    x = (codes.astype(jnp.float32).reshape(rows, nblk, width // nblk) * scales[:, :, None]).reshape(
        rows, width
    )
    inv = lax.rsqrt(jnp.mean(x * x, axis=1, keepdims=True) + 1e-06)
    return (x * inv).astype(jnp.bfloat16)


def make_fold(queries, qtags, query_index):
    width = queries.shape[1]

    def accumulate(carry, piece, start):
        keys, ktags = piece
        member_count = keys.shape[0]
        sims = (
            lax.dot_general(
                queries, keys, (((1,), (1,)), ((), ())), preferred_element_type=jnp.float32
            )
            / width
        )
        key_index = jnp.arange(member_count, dtype=jnp.int32)
        keep = (
            (qtags[:, None] == ktags[None, :])
            & (qtags[:, None] >= 0)
            & (query_index[:, None] != key_index[None, :])
        )
        weights = jnp.where(keep, jnp.exp(8.0 * (sims - 1.0)), jnp.float32(0.0))
        den_sum = jnp.sum(weights, axis=1)
        numerator_sum = jnp.dot(
            weights.astype(jnp.bfloat16), keys, preferred_element_type=jnp.float32
        )
        return (den_sum, numerator_sum)

    return accumulate


def local(codes, scales, cluster_id):
    rows, width = codes.shape
    groups = lax.axis_size("grp")
    member = lax.axis_index("mem")
    embedding_rows = embed(codes, scales)
    owner = cluster_id % groups
    onehot = (owner[:, None] == jnp.arange(groups, dtype=jnp.int32)[None, :]).astype(jnp.int32)
    ranks = jnp.cumsum(onehot, axis=0) - 1
    slot = jnp.sum(ranks * onehot, axis=1)
    target = owner * CAP + slot
    outbox = (
        jnp.zeros((groups * CAP, width), jnp.bfloat16)
        .at[target]
        .set(embedding_rows)
        .reshape(groups, CAP, width)
    )
    outtags = (
        jnp.full((groups * CAP,), -1.0, jnp.float32)
        .at[target]
        .set(cluster_id.astype(jnp.float32))
        .astype(jnp.bfloat16)
        .reshape(groups, CAP)
    )
    slots = groups * CAP
    inbox, incoming_tags = (
        lax.all_to_all(outbox, "grp", split_axis=0, concat_axis=0, tiled=True),
        lax.all_to_all(outtags, "grp", split_axis=0, concat_axis=0, tiled=True),
    )
    queries = inbox.reshape(slots, width)
    qtags = incoming_tags.reshape(slots)
    start_carry = (jnp.zeros((slots,), jnp.float32), jnp.zeros((slots, width), jnp.float32))
    query_index = member * slots + jnp.arange(slots, dtype=jnp.int32)
    accumulate = make_fold(queries, qtags, query_index)
    den_sum, numerator_sum = accumulate(
        start_carry,
        (
            lax.all_gather(queries, "mem", axis=0, tiled=True),
            lax.all_gather(qtags, "mem", axis=0, tiled=True),
        ),
        jnp.int32(0),
    )
    den = 1.0 + den_sum
    result = ((queries.astype(jnp.float32) + numerator_sum) / den[:, None]).astype(jnp.bfloat16)
    mass = jnp.log(den).astype(jnp.bfloat16)
    back_rows, back_mass = (
        lax.all_to_all(
            result.reshape(groups, CAP, width), "grp", split_axis=0, concat_axis=0, tiled=True
        ),
        lax.all_to_all(mass.reshape(groups, CAP), "grp", split_axis=0, concat_axis=0, tiled=True),
    )
    smoothed = back_rows.reshape(slots, width)[target]
    dup_mass = back_mass.reshape(slots)[target]
    return (smoothed, dup_mass)


def solution(mesh):
    placed = (P(("grp", "mem"), None), P(("grp", "mem"), None), P(("grp", "mem")))
    return jax.shard_map(
        local,
        mesh=mesh,
        in_specs=placed,
        out_specs=(P(("grp", "mem"), None), P(("grp", "mem"))),
        check_vma=False,
    )
```

profile of v0, /device:TPU:0, one launch (start us, length us, event | category | flops | bytes accessed | tf_op | source)
XLA Modules:
  0.0 107.8 jit_solution(3126384838830802530)
XLA Ops:
  7.2 0.0 copy-start.1
  7.2 0.0 all-gather.2.cloned.1.call-start
  7.2 0.8 fusion.14
  8.0 0.6 reduce-window.6
  8.6 0.2 slice_reduce_fusion
  8.8 0.1 fusion.9
  8.9 0.8 copy.7
  9.8 0.3 mul.43
  10.1 0.3 multiply_reduce_fusion
  10.4 0.0 copy-start.3
  10.4 2.0 %scatter_custom_fusion = bf16[320,1024]{1,0:T(8,128)(2,1)S(1)} fusion(s32[256]{0:T(256)S(1)} %compare_select_fusion, f32[32,8,8,128]{3,2,1,0:T(8,128)S(1)} %bitcast.26, bf16[256,1024]{1,0:T(8,128)(2,1)S(1)} %copy-done.1, f32[256]{0:T(256)S(1)} %add_rsqrt_fusion, bf16[]{:T(256)} %constant.16.clone.1), kind=kCustom, calls=%fused_computation.17 | custom fusion | flops 1048576 | bytes 2229250 | tf_op jit(solution)/shard_map/scatter | solution.py:60
  12.4 24.9 %all_to_all.26 = bf16[8,40,1024]{2,1,0:T(8,128)(2,1)} all-to-all(bf16[8,40,1024]{2,1,0:T(8,128)(2,1)S(1)} %bitcast.30), channel_id=1, replica_groups=mesh['grp'=8,'mem'=4] {'grp'}, dimensions={0} | all-to-all | bytes 1310720 | tf_op jit(solution)/shard_map/all_to_all | solution.py:72
  37.3 0.0 all-gather.2.cloned.1.call-update
  37.3 1.4 %scatter_custom_fusion.1 = f32[320]{0:T(512)S(1)} fusion(s32[256]{0:T(256)S(1)} %compare_select_fusion, f32[256]{0:T(256)S(1)} %get-tuple-element.4, f32[]{:T(128)} %constant.49.clone.1), kind=kCustom, calls=%fused_computation.35 | custom fusion | bytes 1284 | tf_op jit(solution)/shard_map/scatter | solution.py:66
  38.7 0.7 all_to_all.21
  39.4 3.3 %all-to-all-start.1 = ((bf16[8,1,40]{2,1,0:T(2,128)(2,1)}), bf16[8,1,40]{2,1,0:T(2,128)(2,1)S(1)}, u32[]{:S(2)}, u32[]{:S(2)}) async-start(bf16[8,1,40]{2,1,0:T(2,128)(2,1)} %all_to_all.21), calls=%async_computation.1 | async-start | bytes 8192 | tf_op jit(solution)/shard_map/all_to_all | solution.py:73
  42.8 0.6 dynamic-slice
  44.0 5.1 %all-to-all-done.1 = bf16[8,1,40]{2,1,0:T(2,128)(2,1)S(1)} async-done(((bf16[8,1,40]{2,1,0:T(2,128)(2,1)}), bf16[8,1,40]{2,1,0:T(2,128)(2,1)S(1)}, u32[]{:S(2)}, u32[]{:S(2)}) %all-to-all-start.1) | async-done | bytes 672 | tf_op jit(solution)/shard_map/all_to_all | solution.py:73
  49.1 0.1 reshape.140
  49.2 0.3 dynamic-update-slice
  49.4 6.1 %all-reduce = bf16[1280]{0:T(1024)(128)(2,1)S(1)} all-reduce(bf16[1280]{0:T(1024)(128)(2,1)S(1)} %dynamic-update-slice), channel_id=1, replica_groups=mesh['grp'=8,'mem'=4] {'mem'}, use_global_device_ids=true, to_apply=%add | all-reduce | flops 1280 | bytes 5120
  55.6 6.2 %all-gather.2.cloned.1.call-done = bf16[1280,1024]{1,0:T(8,128)(2,1)} async-done(((bf16[320,1024]{1,0:T(8,128)(2,1)}), bf16[1280,1024]{1,0:T(8,128)(2,1)}) %all-gather.2.cloned.1.call-update) | async-done | bytes 2621456 | tf_op jit(solution)/shard_map/all_gather | solution.py:83
  61.8 4.5 %fusion.15 = (f32[320]{0:T(512)S(1)}, bf16[320,1280]{1,0:T(8,128)(2,1)}) fusion(bf16[320,1024]{1,0:T(8,128)(2,1)} %bitcast.28, bf16[1280,1024]{1,0:T(8,128)(2,1)} %all-gather.2.cloned.1.call-done, s32[320]{0:T(512)S(1)} %iota_add_fusion, pred[320]{0:T(512)(128)(4,1)S(1)} %broadcast_compare_fusion, bf16[1280]{0:T(1024)(128)(2,1)S(1)} %all-reduce, ...), kind=kOutput, calls=%fused_computation.40 | convolution fusion | flops 843775680 | bytes 4102080 | tf_op jit(solution)/shard_map/dot_general | solution.py:26
  66.3 0.7 convert_element_type.50
  67.0 5.5 %all-to-all-start.3 = ((bf16[8,1,40]{2,1,0:T(2,128)(2,1)}), bf16[8,1,40]{2,1,0:T(2,128)(2,1)S(1)}, u32[]{:S(2)}, u32[]{:S(2)}) async-start(bf16[8,1,40]{2,1,0:T(2,128)(2,1)} %convert_element_type.50), calls=%async_computation.3 | async-start | bytes 8192 | tf_op jit(solution)/shard_map/all_to_all | solution.py:95
  72.5 3.1 %divide_convert_fusion = bf16[320,1024]{1,0:T(8,128)(2,1)} fusion(bf16[1280,1024]{1,0:T(8,128)(2,1)S(1)} %copy-done.2, bf16[320,1024]{1,0:T(8,128)(2,1)S(1)} %bitcast.29, bf16[320,1280]{1,0:T(8,128)(2,1)} %get-tuple-element.7, f32[320]{0:T(512)S(1)} %get-tuple-element.3), kind=kOutput, calls=%fused_computation.12 | convolution fusion | flops 840171520 | bytes 4752640 | tf_op jit(solution)/shard_map/dot_general | solution.py:39
  75.6 3.3 %all-to-all-done.3 = bf16[8,1,40]{2,1,0:T(2,128)(2,1)S(1)} async-done(((bf16[8,1,40]{2,1,0:T(2,128)(2,1)}), bf16[8,1,40]{2,1,0:T(2,128)(2,1)S(1)}, u32[]{:S(2)}, u32[]{:S(2)}) %all-to-all-start.3) | async-done | bytes 672 | tf_op jit(solution)/shard_map/all_to_all | solution.py:95
  78.9 3.5 %all-to-all-start.2 = ((bf16[8,40,1024]{2,1,0:T(8,128)(2,1)}), bf16[8,40,1024]{2,1,0:T(8,128)(2,1)S(1)}, u32[]{:S(2)}, u32[]{:S(2)}) async-start(bf16[8,40,1024]{2,1,0:T(8,128)(2,1)} %bitcast.6), calls=%async_computation.2 | async-start | bytes 1310720 | tf_op jit(solution)/shard_map/all_to_all | solution.py:92
  82.5 0.1 reshape.103
  82.6 2.5 %gather_fusion.1 = bf16[256]{0:T(256)(128)(2,1)} fusion(bf16[320]{0:T(512)(128)(2,1)S(1)} %reshape.103, s32[1024]{0:T(1024)S(1)} %pad_clamp_fusion), kind=kCustom, calls=%fused_computation.1 | custom fusion | bytes 2048 | tf_op jit(solution)/shard_map/gather | solution.py:98
  85.0 13.9 %all-to-all-done.2 = bf16[8,40,1024]{2,1,0:T(8,128)(2,1)S(1)} async-done(((bf16[8,40,1024]{2,1,0:T(8,128)(2,1)}), bf16[8,40,1024]{2,1,0:T(8,128)(2,1)S(1)}, u32[]{:S(2)}, u32[]{:S(2)}) %all-to-all-start.2) | async-done | bytes 655392 | tf_op jit(solution)/shard_map/all_to_all | solution.py:92
  98.9 2.0 %gather_fusion = bf16[256,1024]{1,0:T(8,128)(2,1)} fusion(bf16[320,1024]{1,0:T(8,128)(2,1)S(1)} %bitcast.24, s32[1024]{0:T(1024)S(1)} %pad_clamp_fusion), kind=kCustom, calls=%fused_computation | custom fusion | bytes 1049600 | tf_op jit(solution)/shard_map/gather | solution.py:97
  (19 shorter events, 0.2 us)
Async XLA Ops:
  7.2 2.9 %copy-start.1 = (bf16[256,1024]{1,0:T(8,128)(2,1)S(1)}, bf16[256,1024]{1,0:T(8,128)(2,1)}, u32[]{:S(2)}) copy-start(bf16[256,1024]{1,0:T(8,128)(2,1)} %param.3) | copy-start | bytes 1572868
  7.2 54.6 %all-gather.2.cloned.1.call-start = ((), (), s32[]{:S(2)}) async-start(), calls=%async_computation.4 | async-start | bytes 3276800 | tf_op jit(solution)/shard_map/all_gather | solution.py:83
  10.4 32.4 %copy-start.3 = (u32[32]{0:T(128)S(1)}, u32[32]{0:T(128)}, u32[]{:S(2)}) copy-start(u32[32]{0:T(128)} %constant.55) | copy-start | bytes 388
  39.4 9.6 %all-to-all-start.1 = ((bf16[8,1,40]{2,1,0:T(2,128)(2,1)}), bf16[8,1,40]{2,1,0:T(2,128)(2,1)S(1)}, u32[]{:S(2)}, u32[]{:S(2)}) async-start(bf16[8,1,40]{2,1,0:T(2,128)(2,1)} %all_to_all.21), calls=%async_computation.1 | async-start | bytes 8192 | tf_op jit(solution)/shard_map/all_to_all | solution.py:73
  55.6 16.9 %copy-start = (bf16[8,40,1024]{2,1,0:T(8,128)(2,1)S(1)}, bf16[8,40,1024]{2,1,0:T(8,128)(2,1)}, u32[]{:S(2)}) copy-start(bf16[8,40,1024]{2,1,0:T(8,128)(2,1)} %all_to_all.26) | copy-start | bytes 1966084
  61.8 10.7 %copy-start.2 = (bf16[1280,1024]{1,0:T(8,128)(2,1)S(1)}, bf16[1280,1024]{1,0:T(8,128)(2,1)}, u32[]{:S(2)}) copy-start(bf16[1280,1024]{1,0:T(8,128)(2,1)} %all-gather.2.cloned.1.call-done) | copy-start | bytes 7864324
  67.0 11.9 %all-to-all-start.3 = ((bf16[8,1,40]{2,1,0:T(2,128)(2,1)}), bf16[8,1,40]{2,1,0:T(2,128)(2,1)S(1)}, u32[]{:S(2)}, u32[]{:S(2)}) async-start(bf16[8,1,40]{2,1,0:T(2,128)(2,1)} %convert_element_type.50), calls=%async_computation.3 | async-start | bytes 8192 | tf_op jit(solution)/shard_map/all_to_all | solution.py:95
  78.9 20.1 %all-to-all-start.2 = ((bf16[8,40,1024]{2,1,0:T(8,128)(2,1)}), bf16[8,40,1024]{2,1,0:T(8,128)(2,1)S(1)}, u32[]{:S(2)}, u32[]{:S(2)}) async-start(bf16[8,40,1024]{2,1,0:T(8,128)(2,1)} %bitcast.6), calls=%async_computation.2 | async-start | bytes 1310720 | tf_op jit(solution)/shard_map/all_to_all | solution.py:92
Sparse Core Ops, SparseCore 0:
  37.4 24.3 all-gather.1
where the time goes:
time: 108 us
  blocking collectives  31 us (29%)
  waiting for transfers between devices  28.5 us (26%)
  between operations  14.8 us (14%)
  starting transfers between devices  12.4 us (11%)
  local copies, waits for them, and re-layouts  9.58 us (9%)
  matrix products  7.54 us (7%)
  other arithmetic  3.82 us (4%)
    all_to_all x1, blocking collectives, local(): lax.all_to_all(outbox, 'grp', split_axis=0, concat_axis=0, tiled=True)  24.9 us
    all_to_all x1, waiting for transfers between devices, local(): lax.all_to_all(result.reshape(groups, CAP, width), 'grp', split_axis=0, c...  13.9 us
    all_gather x1, waiting for transfers between devices, local(): lax.all_gather(queries, 'mem', axis=0, tiled=True)  6.2 us
    unnamed x1, blocking collectives  6.14 us
    all_to_all x1, starting transfers between devices, local(): lax.all_to_all(mass.reshape(groups, CAP), 'grp', split_axis=0, concat_axi...  5.52 us
    all_to_all x1, waiting for transfers between devices, local(): lax.all_to_all(outtags, 'grp', split_axis=0, concat_axis=0, tiled=True)  5.05 us
    dot_general x1, matrix products, accumulate(): lax.dot_general(queries, keys, (((1,), (1,)), ((), ())), preferred_elemen...  4.49 us
    all_to_all x1, starting transfers between devices, local(): lax.all_to_all(result.reshape(groups, CAP, width), 'grp', split_axis=0, c...  3.54 us
  transfers between devices with their start and end apart: 4, of which 4 were waited for; matrix products, arithmetic and copies ran while one was open for 7% of the time, Pallas kernels for 0%

commit v1 on v0

--- a/solution.py
+++ b/solution.py
@@ -4,6 +4,18 @@
 from jax.sharding import PartitionSpec as P
 
 CAP = 40
+
+
+def rotated_exchange(shard, axis, split, join):
+    ways, here = (lax.axis_size(axis), lax.axis_index(axis))
+    width = shard.shape[split] // ways
+    turned = jnp.roll(shard, -here * width, axis=split)
+    got = [lax.slice_in_dim(turned, 0, width, axis=split)]
+    for far in range(1, ways):
+        sent = lax.slice_in_dim(turned, far * width, (far + 1) * width, axis=split)
+        got.append(lax.ppermute(sent, axis, [(d, (d + far) % ways) for d in range(ways)]))
+    line = jnp.concatenate(got[::-1], axis=join)
+    return jnp.roll(line, (here + 1) * got[0].shape[join], axis=join)
 
 
 def embed(codes, scales):
@@ -89,9 +101,7 @@
     result = ((queries.astype(jnp.float32) + numerator_sum) / den[:, None]).astype(jnp.bfloat16)
     mass = jnp.log(den).astype(jnp.bfloat16)
     back_rows, back_mass = (
-        lax.all_to_all(
-            result.reshape(groups, CAP, width), "grp", split_axis=0, concat_axis=0, tiled=True
-        ),
+        rotated_exchange(result.reshape(groups, CAP, width), "grp", 0, 0),
         lax.all_to_all(mass.reshape(groups, CAP), "grp", split_axis=0, concat_axis=0, tiled=True),
     )
     smoothed = back_rows.reshape(slots, width)[target]

time: 108 us -> 103 us (0.954)
  waiting for transfers between devices: 28.5 us -> 17.1 us
  starting transfers between devices: 12.4 us -> 21.1 us
  matrix products: 7.54 us -> 4.72 us
    ppermute x0 -> x7, starting transfers between devices: none -> 14.5 us  [rotated_exchange(): lax.ppermute(sent, axis, [(d, (d + far) % ways) for d in range(ways)])]
    all_to_all x1 -> x0, waiting for transfers between devices: 13.9 us -> none  [local(): lax.all_to_all(result.reshape(groups, CAP, width), 'grp', split_axis=0, c...]
    ppermute x0 -> x7, waiting for transfers between devices: none -> 5.84 us  [rotated_exchange(): lax.ppermute(sent, axis, [(d, (d + far) % ways) for d in range(ways)])]
    all_to_all x1 -> x0, starting transfers between devices: 3.54 us -> none  [local(): lax.all_to_all(result.reshape(groups, CAP, width), 'grp', split_axis=0, c...]
    all_to_all x1, waiting for transfers between devices: 3.32 us -> 0.01 us  [local(): lax.all_to_all(mass.reshape(groups, CAP), 'grp', split_axis=0, concat_axi...]
    all_to_all x1, starting transfers between devices: 5.52 us -> 3.31 us  [local(): lax.all_to_all(mass.reshape(groups, CAP), 'grp', split_axis=0, concat_axi...]
    dot_general x1, matrix products: 3.05 us -> 1.04 us  [accumulate(): jnp.dot(weights.astype(jnp.bfloat16), keys, preferred_element_type=jnp.fl...]
  transfers between devices with their start and end apart: 4 -> 10, of which waited for: 4 -> 4; matrix products, arithmetic and copies ran while one was open for 7% -> 5% of each run, Pallas kernels for 0% -> 0%
where the time goes in v1:
time: 103 us
  blocking collectives  31 us (30%)
  starting transfers between devices  21.1 us (20%)
  waiting for transfers between devices  17.1 us (17%)
  between operations  15 us (15%)
  local copies, waits for them, and re-layouts  9.67 us (9%)
  matrix products  4.72 us (5%)
  other arithmetic  4.33 us (4%)
    all_to_all x1, blocking collectives, local(): lax.all_to_all(outbox, 'grp', split_axis=0, concat_axis=0, tiled=True)  24.9 us
    ppermute x7, starting transfers between devices, rotated_exchange(): lax.ppermute(sent, axis, [(d, (d + far) % ways) for d in range(ways)])  14.5 us
    all_gather x1, waiting for transfers between devices, local(): lax.all_gather(queries, 'mem', axis=0, tiled=True)  6.2 us
    unnamed x1, blocking collectives  6.14 us
    ppermute x7, waiting for transfers between devices, rotated_exchange(): lax.ppermute(sent, axis, [(d, (d + far) % ways) for d in range(ways)])  5.84 us
    all_to_all x1, waiting for transfers between devices, local(): lax.all_to_all(outtags, 'grp', split_axis=0, concat_axis=0, tiled=True)  5.02 us
    dot_general x1, matrix products, accumulate(): lax.dot_general(queries, keys, (((1,), (1,)), ((), ())), preferred_elemen...  3.68 us
    all_to_all x1, starting transfers between devices, local(): lax.all_to_all(outtags, 'grp', split_axis=0, concat_axis=0, tiled=True)  3.31 us
  transfers between devices with their start and end apart: 10, of which 4 were waited for; matrix products, arithmetic and copies ran while one was open for 5% of the time, Pallas kernels for 0%

profile of v1, /device:TPU:0, one launch (start us, length us, event | category | flops | bytes accessed | tf_op | source)
XLA Modules:
  0.0 103.0 jit_solution(16545108151875446343)
XLA Ops:
  7.2 0.8 fusion.17
  8.0 0.6 reduce-window.6
  8.6 0.2 slice_reduce_fusion
  8.9 0.8 copy.7
  9.8 0.3 mul.43
  10.1 0.3 multiply_reduce_fusion
  10.4 2.0 %scatter_custom_fusion = bf16[320,1024]{1,0:T(8,128)(2,1)S(1)} fusion(s32[256]{0:T(256)S(1)} %compare_select_fusion, f32[32,8,8,128]{3,2,1,0:T(8,128)S(1)} %bitcast.26, bf16[256,1024]{1,0:T(8,128)(2,1)S(1)} %copy-done.1, f32[256]{0:T(256)S(1)} %add_rsqrt_fusion, bf16[]{:T(256)} %constant.60.clone.1), kind=kCustom, calls=%fused_computation.23 | custom fusion | flops 1048576 | bytes 2229250 | tf_op jit(solution)/shard_map/scatter | solution.py:72
  12.4 24.9 %all_to_all.21 = bf16[8,40,1024]{2,1,0:T(8,128)(2,1)} all-to-all(bf16[8,40,1024]{2,1,0:T(8,128)(2,1)S(1)} %bitcast.30), channel_id=1, replica_groups=mesh['grp'=8,'mem'=4] {'grp'}, dimensions={0} | all-to-all | bytes 1310720 | tf_op jit(solution)/shard_map/all_to_all | solution.py:84
  37.3 1.4 %scatter_custom_fusion.1 = f32[320]{0:T(512)S(1)} fusion(s32[256]{0:T(256)S(1)} %compare_select_fusion, f32[256]{0:T(256)S(1)} %get-tuple-element.12, f32[]{:T(128)} %constant.70.clone.1), kind=kCustom, calls=%fused_computation.49 | custom fusion | bytes 1284 | tf_op jit(solution)/shard_map/scatter | solution.py:78
  38.7 0.7 all_to_all.17
  39.4 3.3 %all-to-all-start.1 = ((bf16[8,1,40]{2,1,0:T(2,128)(2,1)}), bf16[8,1,40]{2,1,0:T(2,128)(2,1)S(1)}, u32[]{:S(2)}, u32[]{:S(2)}) async-start(bf16[8,1,40]{2,1,0:T(2,128)(2,1)} %all_to_all.17), calls=%async_computation.1 | async-start | bytes 8192 | tf_op jit(solution)/shard_map/all_to_all | solution.py:85
  42.8 0.6 dynamic-slice
  44.0 5.0 %all-to-all-done.1 = bf16[8,1,40]{2,1,0:T(2,128)(2,1)S(1)} async-done(((bf16[8,1,40]{2,1,0:T(2,128)(2,1)}), bf16[8,1,40]{2,1,0:T(2,128)(2,1)S(1)}, u32[]{:S(2)}, u32[]{:S(2)}) %all-to-all-start.1) | async-done | bytes 672 | tf_op jit(solution)/shard_map/all_to_all | solution.py:85
  49.2 0.3 dynamic-update-slice
  49.4 6.1 %all-reduce = bf16[1280]{0:T(1024)(128)(2,1)S(1)} all-reduce(bf16[1280]{0:T(1024)(128)(2,1)S(1)} %dynamic-update-slice), channel_id=1, replica_groups=mesh['grp'=8,'mem'=4] {'mem'}, use_global_device_ids=true, to_apply=%add | all-reduce | flops 1280 | bytes 5120
  55.6 6.2 %all-gather.2.cloned.1.call-done = bf16[1280,1024]{1,0:T(8,128)(2,1)} async-done(((bf16[320,1024]{1,0:T(8,128)(2,1)}), bf16[1280,1024]{1,0:T(8,128)(2,1)}) %all-gather.2.cloned.1.call-update) | async-done | bytes 2621456 | tf_op jit(solution)/shard_map/all_gather | solution.py:95
  61.8 3.7 %fusion.18 = (f32[320]{0:T(512)S(1)}, bf16[320,1280]{1,0:T(8,128)(2,1)S(1)}) fusion(bf16[320,1024]{1,0:T(8,128)(2,1)} %bitcast.28, bf16[1280,1024]{1,0:T(8,128)(2,1)} %all-gather.2.cloned.1.call-done, s32[320]{0:T(512)S(1)} %iota_add_fusion, pred[320]{0:T(512)(128)(4,1)S(1)} %broadcast_compare_fusion, bf16[1280]{0:T(1024)(128)(2,1)S(1)} %all-reduce, ...), kind=kOutput, calls=%fused_computation.55 | convolution fusion | flops 843775680 | bytes 4102080 | tf_op jit(solution)/shard_map/dot_general | solution.py:38
  65.5 1.0 %divide_convert_fusion = bf16[320,1024]{1,0:T(8,128)(2,1)S(1)} fusion(bf16[1280,1024]{1,0:T(8,128)(2,1)S(1)} %copy-done.2, bf16[320,1024]{1,0:T(8,128)(2,1)S(1)} %bitcast.29, bf16[320,1280]{1,0:T(8,128)(2,1)S(1)} %get-tuple-element.15, f32[320]{0:T(512)S(1)} %get-tuple-element.11), kind=kOutput, calls=%fused_computation.16 | convolution fusion | flops 840171520 | bytes 4752640 | tf_op jit(solution)/shard_map/dot_general | solution.py:51
  66.6 0.3 fusion.7
  66.9 4.3 %collective-permute-start = (bf16[1,40,1024]{2,1,0:T(8,128)(2,1)S(1)}, bf16[1,40,1024]{2,1,0:T(8,128)(2,1)S(1)}, u32[]{:S(2)}, u32[]{:S(2)}) collective-permute-start(bf16[1,40,1024]{2,1,0:T(8,128)(2,1)S(1)} %get-tuple-element.9), channel_id=1, source_target_pairs={{0,28},{4,0},{8,4},{12,8},{16,12},{20,16},{24,20},{28,24},{1,29},{... | collective-permute-start | bytes 245768 | tf_op jit(solution)/shard_map/ppermute | solution.py:16
  71.2 0.7 convert_element_type.50
  71.8 3.3 %all-to-all-start.2 = ((bf16[8,1,40]{2,1,0:T(2,128)(2,1)}), bf16[8,1,40]{2,1,0:T(2,128)(2,1)S(1)}, u32[]{:S(2)}, u32[]{:S(2)}) async-start(bf16[8,1,40]{2,1,0:T(2,128)(2,1)} %convert_element_type.50), calls=%async_computation.2 | async-start | bytes 8192 | tf_op jit(solution)/shard_map/all_to_all | solution.py:105
  75.2 3.7 %collective-permute-start.1 = (bf16[1,40,1024]{2,1,0:T(8,128)(2,1)S(1)}, bf16[1,40,1024]{2,1,0:T(8,128)(2,1)S(1)}, u32[]{:S(2)}, u32[]{:S(2)}) collective-permute-start(bf16[1,40,1024]{2,1,0:T(8,128)(2,1)S(1)} %get-tuple-element.8), channel_id=1, source_target_pairs={{0,24},{4,28},{8,0},{12,4},{16,8},{20,12},{24,16},{28,20},{1,25},{... | collective-permute-start | bytes 245768 | tf_op jit(solution)/shard_map/ppermute | solution.py:16
  78.9 0.5 collective-permute-start.2
  79.5 3.3 %collective-permute-start.3 = (bf16[1,40,1024]{2,1,0:T(8,128)(2,1)S(1)}, bf16[1,40,1024]{2,1,0:T(8,128)(2,1)S(1)}, u32[]{:S(2)}, u32[]{:S(2)}) collective-permute-start(bf16[1,40,1024]{2,1,0:T(8,128)(2,1)S(1)} %get-tuple-element.6), channel_id=1, source_target_pairs={{0,16},{4,20},{8,24},{12,28},{16,0},{20,4},{24,8},{28,12},{1,17},{... | collective-permute-start | bytes 245768 | tf_op jit(solution)/shard_map/ppermute | solution.py:16
  82.9 2.5 %gather_fusion.1 = bf16[256]{0:T(256)(128)(2,1)} fusion(bf16[320]{0:T(512)(128)(2,1)S(1)} %reshape.103, s32[1024]{0:T(1024)S(1)} %pad_clamp_fusion), kind=kCustom, calls=%fused_computation.1 | custom fusion | bytes 2048 | tf_op jit(solution)/shard_map/gather | solution.py:108
  85.3 1.1 %collective-permute-start.5 = (bf16[1,40,1024]{2,1,0:T(8,128)(2,1)S(1)}, bf16[1,40,1024]{2,1,0:T(8,128)(2,1)S(1)}, u32[]{:S(2)}, u32[]{:S(2)}) collective-permute-start(bf16[1,40,1024]{2,1,0:T(8,128)(2,1)S(1)} %get-tuple-element.4), channel_id=1, source_target_pairs={{0,8},{4,12},{8,16},{12,20},{16,24},{20,28},{24,0},{28,4},{1,9},{5... | collective-permute-start | bytes 245768 | tf_op jit(solution)/shard_map/ppermute | solution.py:16
  86.4 1.5 %collective-permute-start.6 = (bf16[1,40,1024]{2,1,0:T(8,128)(2,1)S(1)}, bf16[1,40,1024]{2,1,0:T(8,128)(2,1)S(1)}, u32[]{:S(2)}, u32[]{:S(2)}) collective-permute-start(bf16[1,40,1024]{2,1,0:T(8,128)(2,1)S(1)} %get-tuple-element.3), channel_id=1, source_target_pairs={{0,4},{4,8},{8,12},{12,16},{16,20},{20,24},{24,28},{28,0},{1,5},{5... | collective-permute-start | bytes 245768 | tf_op jit(solution)/shard_map/ppermute | solution.py:16
  88.0 4.3 %collective-permute-done.3 = bf16[1,40,1024]{2,1,0:T(8,128)(2,1)S(1)} collective-permute-done((bf16[1,40,1024]{2,1,0:T(8,128)(2,1)S(1)}, bf16[1,40,1024]{2,1,0:T(8,128)(2,1)S(1)}, u32[]{:S(2)}, u32[]{:S(2)}) %collective-permute-start.3) | collective-permute-done | bytes 81952 | tf_op jit(solution)/shard_map/ppermute | solution.py:16
  92.3 1.5 %collective-permute-done.4 = bf16[1,40,1024]{2,1,0:T(8,128)(2,1)S(1)} collective-permute-done((bf16[1,40,1024]{2,1,0:T(8,128)(2,1)S(1)}, bf16[1,40,1024]{2,1,0:T(8,128)(2,1)S(1)}, u32[]{:S(2)}, u32[]{:S(2)}) %collective-permute-start.4) | collective-permute-done | bytes 81952 | tf_op jit(solution)/shard_map/ppermute | solution.py:16
  93.9 0.3 fusion.6
  94.1 2.0 %gather_fusion = bf16[256,1024]{1,0:T(8,128)(2,1)} fusion(bf16[320,1024]{1,0:T(8,128)(2,1)S(1)} %bitcast.24, s32[1024]{0:T(1024)S(1)} %pad_clamp_fusion), kind=kCustom, calls=%fused_computation | custom fusion | bytes 1049600 | tf_op jit(solution)/shard_map/gather | solution.py:107
  (42 shorter events, 0.6 us)
Async XLA Ops:
  7.2 2.9 %copy-start.1 = (bf16[256,1024]{1,0:T(8,128)(2,1)S(1)}, bf16[256,1024]{1,0:T(8,128)(2,1)}, u32[]{:S(2)}) copy-start(bf16[256,1024]{1,0:T(8,128)(2,1)} %param.5) | copy-start | bytes 1572868
  7.2 54.6 %all-gather.2.cloned.1.call-start = ((), (), s32[]{:S(2)}) async-start(), calls=%async_computation.3 | async-start | bytes 3276800 | tf_op jit(solution)/shard_map/all_gather | solution.py:95
  10.4 32.4 %copy-start.3 = (u32[32]{0:T(128)S(1)}, u32[32]{0:T(128)}, u32[]{:S(2)}) copy-start(u32[32]{0:T(128)} %constant.79) | copy-start | bytes 388
  39.4 9.6 %all-to-all-start.1 = ((bf16[8,1,40]{2,1,0:T(2,128)(2,1)}), bf16[8,1,40]{2,1,0:T(2,128)(2,1)S(1)}, u32[]{:S(2)}, u32[]{:S(2)}) async-start(bf16[8,1,40]{2,1,0:T(2,128)(2,1)} %all_to_all.17), calls=%async_computation.1 | async-start | bytes 8192 | tf_op jit(solution)/shard_map/all_to_all | solution.py:85
  55.6 9.9 %copy-start = (bf16[8,40,1024]{2,1,0:T(8,128)(2,1)S(1)}, bf16[8,40,1024]{2,1,0:T(8,128)(2,1)}, u32[]{:S(2)}) copy-start(bf16[8,40,1024]{2,1,0:T(8,128)(2,1)} %all_to_all.21) | copy-start | bytes 1966084
  61.8 3.7 %copy-start.2 = (bf16[1280,1024]{1,0:T(8,128)(2,1)S(1)}, bf16[1280,1024]{1,0:T(8,128)(2,1)}, u32[]{:S(2)}) copy-start(bf16[1280,1024]{1,0:T(8,128)(2,1)} %all-gather.2.cloned.1.call-done) | copy-start | bytes 7864324
  66.9 18.5 %collective-permute-start = (bf16[1,40,1024]{2,1,0:T(8,128)(2,1)S(1)}, bf16[1,40,1024]{2,1,0:T(8,128)(2,1)S(1)}, u32[]{:S(2)}, u32[]{:S(2)}) collective-permute-start(bf16[1,40,1024]{2,1,0:T(8,128)(2,1)S(1)} %get-tuple-element.9), channel_id=1, source_target_pairs={{0,28},{4,0},{8,4},{12,8},{16,12},{20,16},{24,20},{28,24},{1,29},{... | collective-permute-start | bytes 245768 | tf_op jit(solution)/shard_map/ppermute | solution.py:16
  71.8 10.9 %all-to-all-start.2 = ((bf16[8,1,40]{2,1,0:T(2,128)(2,1)}), bf16[8,1,40]{2,1,0:T(2,128)(2,1)S(1)}, u32[]{:S(2)}, u32[]{:S(2)}) async-start(bf16[8,1,40]{2,1,0:T(2,128)(2,1)} %convert_element_type.50), calls=%async_computation.2 | async-start | bytes 8192 | tf_op jit(solution)/shard_map/all_to_all | solution.py:105
  75.2 11.3 %collective-permute-start.1 = (bf16[1,40,1024]{2,1,0:T(8,128)(2,1)S(1)}, bf16[1,40,1024]{2,1,0:T(8,128)(2,1)S(1)}, u32[]{:S(2)}, u32[]{:S(2)}) collective-permute-start(bf16[1,40,1024]{2,1,0:T(8,128)(2,1)S(1)} %get-tuple-element.8), channel_id=1, source_target_pairs={{0,24},{4,28},{8,0},{12,4},{16,8},{20,12},{24,16},{28,20},{1,25},{... | collective-permute-start | bytes 245768 | tf_op jit(solution)/shard_map/ppermute | solution.py:16
  78.9 9.1 %collective-permute-start.2 = (bf16[1,40,1024]{2,1,0:T(8,128)(2,1)S(1)}, bf16[1,40,1024]{2,1,0:T(8,128)(2,1)S(1)}, u32[]{:S(2)}, u32[]{:S(2)}) collective-permute-start(bf16[1,40,1024]{2,1,0:T(8,128)(2,1)S(1)} %get-tuple-element.7), channel_id=1, source_target_pairs={{0,20},{4,24},{8,28},{12,0},{16,4},{20,8},{24,12},{28,16},{1,21},{... | collective-permute-start | bytes 245768 | tf_op jit(solution)/shard_map/ppermute | solution.py:16
  79.5 12.8 %collective-permute-start.3 = (bf16[1,40,1024]{2,1,0:T(8,128)(2,1)S(1)}, bf16[1,40,1024]{2,1,0:T(8,128)(2,1)S(1)}, u32[]{:S(2)}, u32[]{:S(2)}) collective-permute-start(bf16[1,40,1024]{2,1,0:T(8,128)(2,1)S(1)} %get-tuple-element.6), channel_id=1, source_target_pairs={{0,16},{4,20},{8,24},{12,28},{16,0},{20,4},{24,8},{28,12},{1,17},{... | collective-permute-start | bytes 245768 | tf_op jit(solution)/shard_map/ppermute | solution.py:16
  82.7 11.1 %collective-permute-start.4 = (bf16[1,40,1024]{2,1,0:T(8,128)(2,1)S(1)}, bf16[1,40,1024]{2,1,0:T(8,128)(2,1)S(1)}, u32[]{:S(2)}, u32[]{:S(2)}) collective-permute-start(bf16[1,40,1024]{2,1,0:T(8,128)(2,1)S(1)} %get-tuple-element.5), channel_id=1, source_target_pairs={{0,12},{4,16},{8,20},{12,24},{16,28},{20,0},{24,4},{28,8},{1,13},{... | collective-permute-start | bytes 245768 | tf_op jit(solution)/shard_map/ppermute | solution.py:16
  85.3 8.5 %collective-permute-start.5 = (bf16[1,40,1024]{2,1,0:T(8,128)(2,1)S(1)}, bf16[1,40,1024]{2,1,0:T(8,128)(2,1)S(1)}, u32[]{:S(2)}, u32[]{:S(2)}) collective-permute-start(bf16[1,40,1024]{2,1,0:T(8,128)(2,1)S(1)} %get-tuple-element.4), channel_id=1, source_target_pairs={{0,8},{4,12},{8,16},{12,20},{16,24},{20,28},{24,0},{28,4},{1,9},{5... | collective-permute-start | bytes 245768 | tf_op jit(solution)/shard_map/ppermute | solution.py:16
  86.4 7.4 %collective-permute-start.6 = (bf16[1,40,1024]{2,1,0:T(8,128)(2,1)S(1)}, bf16[1,40,1024]{2,1,0:T(8,128)(2,1)S(1)}, u32[]{:S(2)}, u32[]{:S(2)}) collective-permute-start(bf16[1,40,1024]{2,1,0:T(8,128)(2,1)S(1)} %get-tuple-element.3), channel_id=1, source_target_pairs={{0,4},{4,8},{8,12},{12,16},{16,20},{20,24},{24,28},{28,0},{1,5},{5... | collective-permute-start | bytes 245768 | tf_op jit(solution)/shard_map/ppermute | solution.py:16
Sparse Core Ops, SparseCore 0:
  37.4 24.3 all-gather.1
